TPU v7x, 32 devices: a whole 2x2x4 slice. The times are simulated.
32 devices in a mesh: group: 4 (over y, core), freq: 8 (over z, x).
Axes of the slice: x: 2, y: 2, z: 4, core: 2. Of those that a mesh axis runs over, the one named last changes fastest.
Arguments:
- spectra: bfloat16 [2048, 2, 16], P('freq', None, 'group'), may hold values from -6 to 6
- templates: bfloat16 [2048, 2, 2560], P('freq', None, 'group'), may hold values from -600 to 600
- valid_start: int32 [16], replicated, may hold values from 0 to 2048
Outputs:
- peaks: float32 [2560, 16], P('group')
All inputs are finite; a program needn't handle non-finite values.
Results may differ from a plain program's by a relative error of at most 0.0019.
Values may be sent and summed in bfloat16 or wider, within the bound.
A program may use at most 256 MiB of HBM per device.

v0:
```python
import math
import jax
import jax.numpy as jnp
from jax import lax
from jax.sharding import PartitionSpec as P

N = 4096
VALID = 2048


def make_table(bins_count, lag_index):
    bins_index = jnp.arange(bins_count, dtype=jnp.int32)
    angle = (bins_index[:, None] * lag_index[None, :] % N).astype(jnp.float32) * (2.0 * math.pi / N)
    cosine = jnp.cos(angle)
    sine_part = jnp.sin(angle)
    upper = jnp.concatenate([cosine, sine_part], 1)
    lower = jnp.concatenate([-sine_part, cosine], 1)
    return jnp.concatenate([upper, lower], 0).astype(jnp.bfloat16)


def make_cross(bank_piece, seg_piece):
    bank_re = bank_piece[:, 0, :].astype(jnp.float32)[:, None, :]
    bank_im = bank_piece[:, 1, :].astype(jnp.float32)[:, None, :]
    seg_re = seg_piece[:, 0, :].astype(jnp.float32)[:, :, None]
    seg_im = seg_piece[:, 1, :].astype(jnp.float32)[:, :, None]
    cross_re = bank_re * seg_re + bank_im * seg_im
    cross_im = bank_re * seg_im - bank_im * seg_re
    joined = jnp.stack([cross_re, cross_im], 0).astype(jnp.bfloat16)
    return joined.reshape(2 * joined.shape[1], joined.shape[2] * joined.shape[3])


def contract(cross, table):
    return lax.dot_general(
        cross, table, (((0,), (0,)), ((), ())), preferred_element_type=jnp.float32
    )


def on_device(spectra, templates, valid_start):
    freq_count = lax.axis_size("freq")
    lag_count = N // freq_count
    lag_index = lax.axis_index("freq") * lag_count + jnp.arange(lag_count, dtype=jnp.int32)
    tpl_rows = templates.shape[2]
    every_segment = lax.all_gather(spectra, "group", axis=2, tiled=True)
    count = every_segment.shape[2]
    bank_piece = lax.all_gather(templates, "freq", axis=0, tiled=True)
    seg_piece = lax.all_gather(every_segment, "freq", axis=0, tiled=True)
    width = bank_piece.shape[0]
    cross = make_cross(bank_piece, seg_piece)
    series = contract(cross, make_table(width, lag_index))
    bank_float = bank_piece.astype(jnp.float32)
    norm_sum = jnp.sum(bank_float * bank_float, axis=(0, 1))
    series, template_norm = (series, norm_sum)
    power = (
        series[:, :lag_count] * series[:, :lag_count]
        + series[:, lag_count:] * series[:, lag_count:]
    )
    power = power.reshape(count, tpl_rows, lag_count) / template_norm[None, :, None]
    inside = (lag_index[None, :] >= valid_start[:, None]) & (
        lag_index[None, :] < valid_start[:, None] + VALID
    )
    peaks = jnp.max(jnp.where(inside[:, None, :], power, jnp.float32(0.0)), axis=2).T
    return lax.pmax(peaks, "freq")


def solution(mesh):
    in_specs = (P("freq", None, "group"), P("freq", None, "group"), P())
    out_specs = P("group", None)
    return jax.shard_map(
        on_device, mesh=mesh, in_specs=in_specs, out_specs=out_specs, check_vma=False
    )
```

profile of v0, /device:TPU:0, one launch (start us, length us, event | category | flops | bytes accessed | tf_op | source)
XLA Modules:
  0.0 411.2 jit_solution(10462110616772859024)
XLA Ops:
  6.5 0.0 all-gather.2.cloned.1.call-start
  6.5 2.0 copy.14
  8.5 0.0 all-gather.2.cloned.1.call-update
  8.6 0.7 copy.15
  9.3 6.3 %all_gather.10 = bf16[256,2,16]{0,1,2:T(2,128)(2,1)S(1)} all-gather(bf16[256,2,4]{0,1,2:T(2,128)(2,1)S(1)} %copy.15), channel_id=1, replica_groups=mesh['group'=4,'freq'=8] {'group'}, dimensions={2}, use_global_device_ids=true | all-gather | bytes 20480 | tf_op jit(solution)/shard_map/all_gather | solution.py:43
  15.5 23.8 %all_gather.11 = bf16[2048,2,16]{0,1,2:T(2,128)(2,1)S(1)} all-gather(bf16[256,2,16]{0,1,2:T(2,128)(2,1)S(1)} %all_gather.10), channel_id=1, replica_groups=mesh['group'=4,'freq'=8] {'freq'}, dimensions={0}, use_global_device_ids=true | all-gather | bytes 147456 | tf_op jit(solution)/shard_map/all_gather | solution.py:46
  39.3 0.2 slice_convert_fusion.1
  39.5 0.3 copy.18
  39.9 0.3 copy.19
  40.2 0.7 broadcast_add_fusion
  40.9 0.7 compare_and_fusion
  41.6 0.2 copy.13
  41.8 2.8 broadcast_in_dim.10
  44.6 5.5 %copy.20 = pred[64,8,16,640]{3,1,2,0:T(8,128)(4,1)} copy(pred[64,8,16,640]{3,2,1,0:T(8,128)(4,1)S(1)} %bitcast.22) | data formatting | bytes 10485760
  50.2 18.7 %fusion.21 = (bf16[2048,512]{1,0:T(8,128)(2,1)}, bf16[2048,512]{1,0:T(8,128)(2,1)}, bf16[2048,512]{1,0:T(8,128)(2,1)}) fusion(s32[512]{0:T(512)S(1)} %iota_add_fusion), kind=kLoop, calls=%fused_computation.34 | loop fusion | flops 18874368 | bytes 6293504 | tf_op jit(solution)/shard_map/convert.9
  68.8 30.4 %all-gather.2.cloned.1.call-done = bf16[2048,2,640]{2,0,1:T(8,128)(2,1)} async-done(((bf16[256,2,640]{2,0,1:T(8,128)(2,1)}), bf16[2048,2,640]{2,0,1:T(8,128)(2,1)}) %all-gather.2.cloned.1.call-update) | async-done | bytes 5242896 | tf_op jit(solution)/shard_map/all_gather | solution.py:45
  99.2 7.2 %fusion.19 = (f32[2048,640]{1,0:T(8,128)}, f32[2048,640]{1,0:T(8,128)}) fusion(bf16[2048,2,640]{2,0,1:T(8,128)(2,1)} %all-gather.2.cloned.1.call-done), kind=kLoop, calls=%fused_computation.32 | loop fusion | flops 2621440 | bytes 15728640 | tf_op jit(solution)/shard_map/mul | solution.py:26
  106.4 31.5 %add_convert_fusion = (bf16[1,2048,16,640]{3,2,1,0:T(8,128)(2,1)}, bf16[1,2048,16,640]{3,2,1,0:T(8,128)(2,1)}) fusion(f32[2048,16]{1,0:T(8,128)S(1)} %bitcast.25, f32[2048,640]{1,0:T(8,128)} %get-tuple-element.8, f32[2048,16]{1,0:T(8,128)S(1)} %bitcast.24, f32[2048,640]{1,0:T(8,128)} %get-tuple-element.7), kind=kLoop, calls=%fused_computation.2 | loop fusion | flops 167772160 | bytes 94633984 | tf_op jit(solution)/shard_map/convert.10
  137.9 56.2 %pad_maximum_fusion = bf16[2,2048,16,640]{3,2,1,0:T(8,128)(2,1)} fusion(bf16[1,2048,16,640]{3,2,1,0:T(8,128)(2,1)} %get-tuple-element.6, bf16[1,2048,16,640]{3,2,1,0:T(8,128)(2,1)} %get-tuple-element.5), kind=kLoop, calls=%fused_computation | loop fusion | flops 41943040 | bytes 167772160 | tf_op jit(solution)/shard_map/stack | solution.py:28
  194.1 0.0 copy-start
  194.1 55.4 %copy.21 = bf16[512,8,16,640]{3,1,2,0:T(8,128)(2,1)} copy(bf16[512,8,16,640]{3,2,1,0:T(8,128)(2,1)} %bitcast.12) | data formatting | bytes 167772160
  249.5 3.6 multiply_reduce_fusion
  253.1 0.6 div.14
  253.7 0.0 copy-done
  253.7 0.0 copy-start.1
  253.7 99.3 %fusion.4 = f32[10240,1024]{0,1:T(8,128)} fusion(bf16[4096,10240]{1,0:T(8,128)(2,1)} %bitcast.13, bf16[2048,512]{1,0:T(8,128)(2,1)} %get-tuple-element.13, bf16[2048,512]{1,0:T(8,128)(2,1)} %get-tuple-element.12, bf16[2048,512]{1,0:T(8,128)(2,1)S(1)} %copy-done), kind=kOutput, calls=%fused_computation.10 | convolution fusion | flops 85932900352 | bytes 132120576 | tf_op jit(solution)/shard_map/dot_general | solution.py:33
  353.0 0.0 copy-done.1
  353.0 15.9 %fusion.3 = f32[10240]{0:T(1024)S(1)} fusion(pred[10240,512]{0,1:T(8,128)(4,1)} %bitcast.23, f32[10240,1024]{0,1:T(8,128)} %fusion.4, f32[10240]{0:T(1024)S(1)} %copy-done.1), kind=kLoop, calls=%fused_computation.8 | loop fusion | flops 31447040 | bytes 47267840 | tf_op jit(solution)/shard_map/reduce_max | solution.py:61
  369.0 35.3 %pmax.7 = f32[640,16]{0,1:T(8,128)} all-reduce(f32[640,16]{0,1:T(8,128)S(1)} %bitcast.26), channel_id=1, replica_groups=mesh['group'=4,'freq'=8] {'freq'}, use_global_device_ids=true, to_apply=%region_2.3 | all-reduce | flops 10240 | bytes 81920 | tf_op jit(solution)/shard_map/pmax | solution.py:62
  (3 shorter events, 0.0 us)
Async XLA Ops:
  6.5 92.7 %all-gather.2.cloned.1.call-start = ((), (), s32[]{:S(2)}) async-start(), calls=%async_computation | async-start | bytes 5898240 | tf_op jit(solution)/shard_map/all_gather | solution.py:45
  194.1 59.7 %copy-start = (bf16[2048,512]{1,0:T(8,128)(2,1)S(1)}, bf16[2048,512]{1,0:T(8,128)(2,1)}, u32[]{:S(2)}) copy-start(bf16[2048,512]{1,0:T(8,128)(2,1)} %get-tuple-element.11) | copy-start | bytes 6291460
  253.7 99.3 %copy-start.1 = (f32[10240]{0:T(1024)S(1)}, f32[10240]{0:T(1024)}, u32[]{:S(2)}) copy-start(f32[10240]{0:T(1024)} %div.14) | copy-start | bytes 122884
Sparse Core Ops, SparseCore 0:
  9.5 89.6 all-gather.1
where the time goes:
time: 411 us
  other arithmetic  135 us (33%)
  matrix products  99.3 us (24%)
  local copies, waits for them, and re-layouts  68 us (17%)
  blocking collectives  65.4 us (16%)
  waiting for transfers between devices  30.4 us (7%)
  between operations  13.5 us (3%)
    dot_general x1, matrix products, contract(): lax.dot_general(cross, table, (((0,), (0,)), ((), ())), preferred_element...  99.3 us
    unnamed x8, local copies, waits for them, and re-layouts  63.7 us
    another operation x1, other arithmetic, make_cross(): joined = jnp.stack([cross_re, cross_im], 0).astype(jnp.bfloat16)  56.2 us
    another operation x2, other arithmetic  50.2 us
    pmax x1, blocking collectives, on_device(): return lax.pmax(peaks, 'freq')  35.3 us
    all_gather x1, waiting for transfers between devices, on_device(): bank_piece = lax.all_gather(templates, 'freq', axis=0, tiled=True)  30.4 us
    all_gather x1, blocking collectives, on_device(): seg_piece = lax.all_gather(every_segment, 'freq', axis=0, tiled=True)  23.8 us
    reduce_max x1, other arithmetic, on_device(): jnp.max(jnp.where(inside[:, None, :], power, jnp.float32(0.0)), axis=2)  15.9 us
  transfers between devices with their start and end apart: 1, of which 1 were waited for; matrix products, arithmetic and copies ran while one was open for 7% of the time, Pallas kernels for 0%

commit v1 on v0

--- a/solution.py
+++ b/solution.py
@@ -3,6 +3,7 @@
 import jax.numpy as jnp
 from jax import lax
 from jax.sharding import PartitionSpec as P
+from jax.lax import all_to_all, axis_size
 
 N = 4096
 VALID = 2048
@@ -42,7 +43,15 @@
     tpl_rows = templates.shape[2]
     every_segment = lax.all_gather(spectra, "group", axis=2, tiled=True)
     count = every_segment.shape[2]
-    bank_piece = lax.all_gather(templates, "freq", axis=0, tiled=True)
+    bank_piece = jnp.concatenate(
+        all_to_all(
+            jnp.stack([templates] * axis_size("freq"), axis=0),
+            axis_name="freq",
+            split_axis=0,
+            concat_axis=0,
+        ),
+        axis=0,
+    )
     seg_piece = lax.all_gather(every_segment, "freq", axis=0, tiled=True)
     width = bank_piece.shape[0]
     cross = make_cross(bank_piece, seg_piece)

time: 411 us -> 471 us (1.15)
  blocking collectives: 65.4 us -> 161 us
  waiting for transfers between devices: 30.4 us -> 0.01 us
  between operations: 13.5 us -> 0.13 us
  starting transfers between devices: 0.01 us -> 7.28 us
    all_gather x1, blocking collectives: 23.8 us -> 114 us  [on_device(): seg_piece = lax.all_gather(every_segment, 'freq', axis=0, tiled=True)]
    all_gather x1 -> x0, waiting for transfers between devices: 30.4 us -> none  [on_device(): bank_piece = lax.all_gather(templates, 'freq', axis=0, tiled=True)]
    all_to_all x0 -> x1, starting transfers between devices: none -> 7.28 us  [on_device(): all_to_all(jnp.stack([templates] * axis_size('freq'), axis=0), axis_name=...]
    pmax x1, blocking collectives: 35.3 us -> 41.8 us  [on_device(): return lax.pmax(peaks, 'freq')]
    unnamed x8 -> x12, local copies, waits for them, and re-layouts: 63.7 us -> 62.1 us
  transfers between devices with their start and end apart: 1 -> 1, of which waited for: 1 -> 0; matrix products, arithmetic and copies ran while one was open for 7% -> 6% of each run, Pallas kernels for 0% -> 0%
where the time goes in v1:
time: 471 us
  blocking collectives  161 us (34%)
  other arithmetic  131 us (28%)
  matrix products  99.3 us (21%)
  local copies, waits for them, and re-layouts  72.3 us (15%)
  starting transfers between devices  7.28 us (2%)
    all_gather x1, blocking collectives, on_device(): seg_piece = lax.all_gather(every_segment, 'freq', axis=0, tiled=True)  114 us
    dot_general x1, matrix products, contract(): lax.dot_general(cross, table, (((0,), (0,)), ((), ())), preferred_element...  99.3 us
    unnamed x12, local copies, waits for them, and re-layouts  62.1 us
    another operation x1, other arithmetic, make_cross(): joined = jnp.stack([cross_re, cross_im], 0).astype(jnp.bfloat16)  56.2 us
    another operation x2, other arithmetic  50.2 us
    pmax x1, blocking collectives, on_device(): return lax.pmax(peaks, 'freq')  41.8 us
    reduce_max x1, other arithmetic, on_device(): jnp.max(jnp.where(inside[:, None, :], power, jnp.float32(0.0)), axis=2)  15.9 us
  transfers between devices with their start and end apart: 1, of which 0 were waited for; matrix products, arithmetic and copies ran while one was open for 6% of the time, Pallas kernels for 0%

profile of v1, /device:TPU:0, one launch (start us, length us, event | category | flops | bytes accessed | tf_op | source)
XLA Modules:
  0.0 470.8 jit_solution(11588537818297493)
XLA Ops:
  0.0 1.2 copy.15
  1.2 0.0 copy-start.2
  1.2 0.0 copy-start.3
  1.2 2.9 stack.5
  4.1 7.3 %all-to-all-start = ((bf16[8,256,2,640]{3,1,2,0:T(8,128)(2,1)}), bf16[8,256,2,640]{3,1,2,0:T(8,128)(2,1)}, u32[]{:S(2)}, u32[]{:S(2)}) async-start(bf16[8,256,2,640]{3,1,2,0:T(8,128)(2,1)} %stack.5), calls=%async_computation | async-start | bytes 10485760 | tf_op jit(solution)/shard_map/all_to_all | solution.py:47
  11.4 0.0 copy-done.2
  11.4 5.2 %all_gather.6 = bf16[256,2,16]{0,1,2:T(2,128)(2,1)S(1)} all-gather(bf16[256,2,4]{0,1,2:T(2,128)(2,1)S(1)} %copy.17), channel_id=1, replica_groups=mesh['group'=4,'freq'=8] {'group'}, dimensions={2}, use_global_device_ids=true | all-gather | bytes 20480 | tf_op jit(solution)/shard_map/all_gather | solution.py:44
  16.6 114.0 %all_gather.7 = bf16[2048,2,16]{0,1,2:T(2,128)(2,1)S(1)} all-gather(bf16[256,2,16]{0,1,2:T(2,128)(2,1)S(1)} %all_gather.6), channel_id=1, replica_groups=mesh['group'=4,'freq'=8] {'freq'}, dimensions={0}, use_global_device_ids=true | all-gather | bytes 147456 | tf_op jit(solution)/shard_map/all_gather | solution.py:55
  130.6 0.2 slice_convert_fusion.1
  130.8 0.3 copy.20
  131.2 0.3 copy.21
  131.5 0.0 copy-done.3
  131.5 0.1 compare_and_fusion
  131.6 0.2 copy.14
  131.8 2.8 broadcast_in_dim.10
  134.7 5.5 %copy.22 = pred[64,8,16,640]{3,1,2,0:T(8,128)(4,1)} copy(pred[64,8,16,640]{3,2,1,0:T(8,128)(4,1)S(1)} %bitcast.23) | data formatting | bytes 10485760
  140.2 18.7 %fusion.21 = (bf16[2048,512]{1,0:T(8,128)(2,1)}, bf16[2048,512]{1,0:T(8,128)(2,1)}, bf16[2048,512]{1,0:T(8,128)(2,1)}) fusion(s32[512]{0:T(512)S(1)} %iota_add_fusion), kind=kLoop, calls=%fused_computation.34 | loop fusion | flops 18874368 | bytes 6293504 | tf_op jit(solution)/shard_map/convert.9
  158.8 0.0 all-to-all-done
  158.8 2.9 copy.16
  161.8 4.6 fusion.19
  166.4 31.5 %add_convert_fusion = (bf16[1,2048,16,640]{3,2,1,0:T(8,128)(2,1)}, bf16[1,2048,16,640]{3,2,1,0:T(8,128)(2,1)}) fusion(f32[2048,16]{1,0:T(8,128)S(1)} %bitcast.27, f32[2048,640]{1,0:T(8,128)} %get-tuple-element.8, f32[2048,16]{1,0:T(8,128)S(1)} %bitcast.26, f32[2048,640]{1,0:T(8,128)} %get-tuple-element.7), kind=kLoop, calls=%fused_computation.2 | loop fusion | flops 167772160 | bytes 94633984 | tf_op jit(solution)/shard_map/convert.10
  197.9 56.2 %pad_maximum_fusion = bf16[2,2048,16,640]{3,2,1,0:T(8,128)(2,1)} fusion(bf16[1,2048,16,640]{3,2,1,0:T(8,128)(2,1)} %get-tuple-element.6, bf16[1,2048,16,640]{3,2,1,0:T(8,128)(2,1)} %get-tuple-element.5), kind=kLoop, calls=%fused_computation | loop fusion | flops 41943040 | bytes 167772160 | tf_op jit(solution)/shard_map/stack | solution.py:29
  254.1 0.0 copy-start
  254.1 55.4 %copy.23 = bf16[512,8,16,640]{3,1,2,0:T(8,128)(2,1)} copy(bf16[512,8,16,640]{3,2,1,0:T(8,128)(2,1)} %bitcast.13) | data formatting | bytes 167772160
  309.6 3.6 multiply_reduce_fusion
  313.1 0.6 div.14
  313.8 0.0 copy-done
  313.8 0.0 copy-start.1
  313.8 99.3 %fusion.4 = f32[10240,1024]{0,1:T(8,128)} fusion(bf16[4096,10240]{1,0:T(8,128)(2,1)} %bitcast.14, bf16[2048,512]{1,0:T(8,128)(2,1)} %get-tuple-element.13, bf16[2048,512]{1,0:T(8,128)(2,1)} %get-tuple-element.12, bf16[2048,512]{1,0:T(8,128)(2,1)S(1)} %copy-done), kind=kOutput, calls=%fused_computation.10 | convolution fusion | flops 85932900352 | bytes 132120576 | tf_op jit(solution)/shard_map/dot_general | solution.py:34
  413.0 0.0 copy-done.1
  413.0 15.9 %fusion.3 = f32[10240]{0:T(1024)S(1)} fusion(pred[10240,512]{0,1:T(8,128)(4,1)} %bitcast.25, f32[10240,1024]{0,1:T(8,128)} %fusion.4, f32[10240]{0:T(1024)S(1)} %copy-done.1), kind=kLoop, calls=%fused_computation.8 | loop fusion | flops 31447040 | bytes 47267840 | tf_op jit(solution)/shard_map/reduce_max | solution.py:70
  429.0 41.8 %pmax.7 = f32[640,16]{0,1:T(8,128)} all-reduce(f32[640,16]{0,1:T(8,128)S(1)} %bitcast.28), channel_id=1, replica_groups=mesh['group'=4,'freq'=8] {'freq'}, use_global_device_ids=true, to_apply=%region_2.3 | all-reduce | flops 10240 | bytes 81920 | tf_op jit(solution)/shard_map/pmax | solution.py:71
  (5 shorter events, 0.0 us)
Async XLA Ops:
  1.2 10.2 %copy-start.2 = (bf16[256,2,4]{0,2,1:T(4,128)(2,1)S(1)}, bf16[256,2,4]{0,2,1:T(4,128)(2,1)}, u32[]{:S(2)}) copy-start(bf16[256,2,4]{0,2,1:T(4,128)(2,1)} %param.3) | copy-start | bytes 12292
  1.2 130.4 %copy-start.3 = (s32[16]{0:T(128)S(1)}, s32[16]{0:T(128)}, u32[]{:S(2)}) copy-start(s32[16]{0:T(128)} %param.5) | copy-start | bytes 196
  4.1 154.7 %all-to-all-start = ((bf16[8,256,2,640]{3,1,2,0:T(8,128)(2,1)}), bf16[8,256,2,640]{3,1,2,0:T(8,128)(2,1)}, u32[]{:S(2)}, u32[]{:S(2)}) async-start(bf16[8,256,2,640]{3,1,2,0:T(8,128)(2,1)} %stack.5), calls=%async_computation | async-start | bytes 10485760 | tf_op jit(solution)/shard_map/all_to_all | solution.py:47
  254.1 59.6 %copy-start = (bf16[2048,512]{1,0:T(8,128)(2,1)S(1)}, bf16[2048,512]{1,0:T(8,128)(2,1)}, u32[]{:S(2)}) copy-start(bf16[2048,512]{1,0:T(8,128)(2,1)} %get-tuple-element.11) | copy-start | bytes 6291460
  313.8 99.3 %copy-start.1 = (f32[10240]{0:T(1024)S(1)}, f32[10240]{0:T(1024)}, u32[]{:S(2)}) copy-start(f32[10240]{0:T(1024)} %div.14) | copy-start | bytes 122884
